TPU v7x, 128 devices: a whole 4x4x4 slice. The times are simulated.
128 devices in a mesh: dp: 16 (over y, x), expert: 8 (over z, core).
Axes of the slice: x: 4, y: 4, z: 4, core: 2. Of those that a mesh axis runs over, the one named last changes fastest.
Arguments:
- tokens: bfloat16 [2048, 2048], P(('dp', 'expert')), may hold values from -6 to 6
- route: int32 [2048, 8], P(('dp', 'expert')), may hold values from 0 to 63, all different within a row; in each aligned block of 16 rows (0 to 15, 16 to 31, ...) at most 2 rows name the same one
- probs: float32 [2048, 8], P(('dp', 'expert')), may hold values from 0.03 to 0.3
- cotangent: bfloat16 [2048, 2048], P(('dp', 'expert')), may hold values from -6 to 6
- gate_weight: bfloat16 [128, 2048, 384], P(('dp', 'expert')), may hold values from -0.125 to 0.125
- up_weight: bfloat16 [128, 2048, 384], P(('dp', 'expert')), may hold values from -0.125 to 0.125
- down_weight: bfloat16 [128, 384, 2048], P(('dp', 'expert')), may hold values from -0.21875 to 0.21875
Outputs:
- mixed: bfloat16 [2048, 2048], P(('dp', 'expert'))
- token_grad: bfloat16 [2048, 2048], P(('dp', 'expert'))
- gate_grad: bfloat16 [128, 2048, 384], P(('dp', 'expert'))
- up_grad: bfloat16 [128, 2048, 384], P(('dp', 'expert'))
- down_grad: bfloat16 [128, 384, 2048], P(('dp', 'expert'))
Inputs may be any that keep to these rules, and one draw needn't show every extreme that they name: `route`: each row names 8 different experts. In each aligned block of 16 rows (the rows of one device) no expert is named by more than 2 rows, a bound that some block reaches.
All inputs are finite; a program needn't handle non-finite values.
Results may differ from a plain program's by a relative error of at most 0.0065.
Values may be sent and summed in bfloat16 or wider, within the bound.
A program may use at most 64 MiB of HBM per device.

v0:
```python
import jax
import jax.numpy as jnp
from jax import lax
from jax.sharding import PartitionSpec as P

TOP = 8


def sent_together(arrays, axis, split_dim, concat_dim, along):
    both = jnp.concatenate(arrays, axis=along)
    result, at, gathered = (
        lax.all_to_all(both, axis, split_axis=split_dim, concat_axis=concat_dim, tiled=True),
        0,
        [],
    )
    for a in arrays:
        gathered.append(lax.slice_in_dim(result, at, at + a.shape[along], axis=along))
        at += a.shape[along]
    return tuple(gathered)


def from_partner(x, axis, apart):
    return lax.ppermute(x, axis, [(i, i ^ 1 << apart) for i in range(lax.axis_size(axis))])


def slot_tables(route_block, prob_block, experts, capacity):
    row_count, top_count = route_block.shape
    flat_ids = route_block.reshape(-1)
    onehot = (flat_ids[:, None] == jnp.arange(experts, dtype=jnp.int32)[None, :]).astype(jnp.int32)
    before = jnp.cumsum(onehot, axis=0) - onehot
    position = jnp.sum(before * onehot, axis=1)
    slot_ids = flat_ids * capacity + position
    matches = (
        slot_ids[:, None] == jnp.arange(experts * capacity, dtype=jnp.int32)[None, :]
    ).astype(jnp.float32)
    matches = matches.reshape(row_count, top_count, experts * capacity)
    return (jnp.sum(matches, axis=1), jnp.sum(matches * prob_block[:, :, None], axis=1))


def contract_last(left, right):
    return lax.dot_general(
        left, right, (((1,), (1,)), ((), ())), preferred_element_type=jnp.float32
    )


def contract_first(left, right):
    return lax.dot_general(
        left, right, (((0,), (0,)), ((), ())), preferred_element_type=jnp.float32
    )


def slice_work(slot_rows, out_cot, w_gate, w_up, w_down):
    gate_val = jnp.dot(slot_rows, w_gate, preferred_element_type=jnp.float32)
    up_val = jnp.dot(slot_rows, w_up, preferred_element_type=jnp.float32)
    sigmoid_val = jax.nn.sigmoid(gate_val)
    act_val = (gate_val * sigmoid_val * up_val).astype(jnp.bfloat16)
    out_part = jnp.dot(act_val, w_down, preferred_element_type=jnp.float32)
    act_cot = contract_last(out_cot, w_down)
    gate_cot = (act_cot * up_val * sigmoid_val * (1.0 + gate_val * (1.0 - sigmoid_val))).astype(
        jnp.bfloat16
    )
    up_cot = (act_cot * gate_val * sigmoid_val).astype(jnp.bfloat16)
    cot_part = contract_last(gate_cot, w_gate) + contract_last(up_cot, w_up)
    grad_gate = contract_first(slot_rows, gate_cot)
    grad_up = contract_first(slot_rows, up_cot)
    grad_down = contract_first(act_val, out_cot)
    return (out_part, cot_part, grad_gate, grad_up, grad_down)


def body(tokens, route, probs, cotangent, gate_weight, up_weight, down_weight):
    highest = lax.Precision.HIGHEST
    devices = lax.axis_size("dp") * lax.axis_size("expert")
    experts = devices // 2
    tok_rows, feature_width = tokens.shape
    capacity = 2 * max(1, 3 * tok_rows * TOP // (4 * experts))
    half_cap = capacity // 2
    spread, weighted = slot_tables(route, probs, experts, capacity)
    spread_half = spread.astype(jnp.bfloat16)
    send_rows = jnp.einsum("ts,td->sd", spread_half, tokens, preferred_element_type=jnp.float32)
    send_rows = send_rows.astype(jnp.bfloat16)
    send_cot = jnp.einsum("ts,td->sd", weighted, cotangent.astype(jnp.float32), precision=highest)
    send_cot = send_cot.astype(jnp.bfloat16)
    w_gate, w_up, w_down = (gate_weight[0], up_weight[0], down_weight[0])
    arrived_rows, arrived_cot = sent_together(
        (
            send_rows.reshape(devices, half_cap, feature_width),
            send_cot.reshape(devices, half_cap, feature_width),
        ),
        ("dp", "expert"),
        0,
        0,
        1,
    )
    own_stack = jnp.stack((arrived_rows, arrived_cot))
    other_stack = from_partner(own_stack, "expert", 0)
    is_lower = lax.axis_index("expert") % 2 == 0
    lower_stack = jnp.where(is_lower, own_stack, other_stack)
    upper_stack = jnp.where(is_lower, other_stack, own_stack)
    joined = jnp.concatenate((lower_stack, upper_stack), axis=2)
    out_part, cot_part, grad_gate, grad_up, grad_down = slice_work(
        joined[0].reshape(-1, feature_width),
        joined[1].reshape(-1, feature_width),
        w_gate,
        w_up,
        w_down,
    )
    part_stack = jnp.stack(
        (
            out_part.reshape(devices, capacity, feature_width),
            cot_part.reshape(devices, capacity, feature_width),
        )
    )
    lower_part = part_stack[:, :, :half_cap]
    upper_part = part_stack[:, :, half_cap:]
    given_part = jnp.where(is_lower, upper_part, lower_part)
    kept_part = jnp.where(is_lower, lower_part, upper_part)
    taken_part = from_partner(given_part, "expert", 0)
    summed = (kept_part + taken_part).astype(jnp.bfloat16)
    back_out, back_cot = sent_together((summed[0], summed[1]), ("dp", "expert"), 0, 0, 1)
    back_out = back_out.reshape(experts, capacity, feature_width)
    back_cot = back_cot.reshape(experts, capacity, feature_width)
    out_rows = back_out.reshape(-1, feature_width)
    rows_cot = back_cot.reshape(-1, feature_width)
    mixed = jnp.einsum(
        "ts,sd->td", weighted, out_rows.astype(jnp.float32), precision=highest
    ).astype(jnp.bfloat16)
    token_grad = jnp.einsum(
        "ts,sd->td", spread_half, rows_cot, preferred_element_type=jnp.float32
    ).astype(jnp.bfloat16)
    return (
        mixed,
        token_grad,
        grad_gate[None].astype(jnp.bfloat16),
        grad_up[None].astype(jnp.bfloat16),
        grad_down[None].astype(jnp.bfloat16),
    )


def solution(mesh):
    in_specs = (
        P(("dp", "expert"), None),
        P(("dp", "expert"), None),
        P(("dp", "expert"), None),
        P(("dp", "expert"), None),
        P(("dp", "expert"), None, None),
        P(("dp", "expert"), None, None),
        P(("dp", "expert"), None, None),
    )
    out_specs = (
        P(("dp", "expert"), None),
        P(("dp", "expert"), None),
        P(("dp", "expert"), None, None),
        P(("dp", "expert"), None, None),
        P(("dp", "expert"), None, None),
    )
    return jax.shard_map(body, mesh=mesh, in_specs=in_specs, out_specs=out_specs, check_vma=False)
```

profile of v0, /device:TPU:1, one launch (start us, length us, event | category | flops | bytes accessed | tf_op | source)
XLA Modules:
  0.0 109.7 jit_solution(7518823032452992217)
XLA Ops:
  0.6 0.0 copy-start
  0.6 0.9 copy.47
  1.5 0.1 eq.34
  1.6 0.1 fusion.18
  1.7 0.2 reduce_window_sum.11
  1.9 0.2 select_reduce_fusion.1
  2.1 0.1 reduce_sum.30
  2.2 0.8 copy.49
  2.9 0.1 convert_reduce_fusion
  3.0 1.2 %fusion.3 = bf16[128,1,2048]{2,0,1:T(8,128)(2,1)S(1)} fusion(bf16[16,2048]{1,0:T(8,128)(2,1)} %param.7, bf16[16,128]{1,0:T(8,128)(2,1)S(1)} %get-tuple-element.5), kind=kOutput, calls=%fused_computation.12 | convolution fusion | flops 8650752 | bytes 593920 | tf_op jit(solution)/shard_map/ts,td->sd/dot_general | solution.py:79
  4.2 1.4 %fusion.4 = bf16[128,1,2048]{2,0,1:T(8,128)(2,1)S(1)} fusion(f32[16,128]{1,0:T(8,128)S(1)} %get-tuple-element.6, bf16[16,2048]{1,0:T(8,128)(2,1)} %param.10), kind=kOutput, calls=%fused_computation.13 | convolution fusion | flops 50593792 | bytes 598016 | tf_op jit(solution)/shard_map/ts,td->sd/dot_general | solution.py:81
  5.7 0.1 pad_maximum_fusion.2
  5.8 1.1 copy.50
  6.9 30.3 %all_to_all.10 = bf16[128,2,2048]{2,1,0:T(2,128)(2,1)S(1)} all-to-all(bf16[128,2,2048]{2,1,0:T(2,128)(2,1)S(1)} %copy.50), channel_id=1, replica_groups=mesh['dp'=16,'expert'=8] {'dp','expert'}, dimensions={0} | all-to-all | bytes 2097152 | tf_op jit(solution)/shard_map/all_to_all | solution.py:12
  37.2 1.5 %fusion.22 = (bf16[128,1,2048]{2,1,0:T(2,128)(2,1)S(1)}, bf16[128,1,2048]{2,1,0:T(2,128)(2,1)S(1)}) fusion(bf16[128,2,2048]{2,1,0:T(2,128)(2,1)S(1)} %all_to_all.10), kind=kLoop, calls=%fused_computation.60 | loop fusion | bytes 2097152 | tf_op jit(solution)/shard_map/slice | solution.py:17
  38.7 0.6 copy_bitcast_fusion.4
  39.3 1.1 pad_maximum_fusion.3
  40.3 1.3 %collective-permute-start = (bf16[2,128,1,2048]{3,1,2,0:T(8,128)(2,1)}, bf16[2,128,1,2048]{3,1,2,0:T(8,128)(2,1)}, u32[]{:S(2)}, u32[]{:S(2)}) collective-permute-start(bf16[2,128,1,2048]{3,1,2,0:T(8,128)(2,1)} %pad_maximum_fusion.3), channel_id=1, source_target_pairs={{0,1},{1,0},{2,3},{3,2},{4,5},{5,4},{6,7},{7,6},{8,9},{9,8},{10,11... | collective-permute-start | bytes 3145736 | tf_op jit(solution)/shard_map/ppermute | solution.py:23
  41.6 2.6 %collective-permute-done = bf16[2,128,1,2048]{3,1,2,0:T(8,128)(2,1)} collective-permute-done((bf16[2,128,1,2048]{3,1,2,0:T(8,128)(2,1)}, bf16[2,128,1,2048]{3,1,2,0:T(8,128)(2,1)}, u32[]{:S(2)}, u32[]{:S(2)}) %collective-permute-start) | collective-permute-done | bytes 1048608 | tf_op jit(solution)/shard_map/ppermute | solution.py:23
  44.3 1.4 %broadcast_select_fusion.1 = (bf16[2,128,1,2048]{3,1,2,0:T(8,128)(2,1)S(1)}, bf16[2,128,1,2048]{3,1,2,0:T(8,128)(2,1)S(1)}) fusion(bf16[2,128,1,2048]{3,1,2,0:T(8,128)(2,1)} %collective-permute-done, pred[]{:T(512)S(6)} %eq.41, bf16[1,128,1,2048]{3,1,2,0:T(8,128)(2,1)S(1)} %get-tuple-element.20, bf16[1,128,1,2048]{3,1,2,0:T(8,128)(2,1)S(1)} %get-tuple-element.21), kind=kLoop, calls=%fused_computation.37 | loop fusion | flops 1572864 | bytes 4194305 | tf_op jit(solution)/shard_map/jit(_where)/select_n | solution.py:98
  45.6 1.2 %pad_maximum_fusion.1 = (bf16[1,128,2,2048]{3,1,2,0:T(8,128)(2,1)}, bf16[1,128,2,2048]{3,1,2,0:T(8,128)(2,1)S(1)}) fusion(bf16[2,128,1,2048]{3,1,2,0:T(8,128)(2,1)S(1)} %get-tuple-element.9, bf16[2,128,1,2048]{3,1,2,0:T(8,128)(2,1)S(1)} %get-tuple-element.10), kind=kLoop, calls=%fused_computation.32 | loop fusion | flops 1048576 | bytes 4194304 | tf_op jit(solution)/shard_map/concatenate | solution.py:99
  46.8 2.0 %copy.53 = bf16[1,128,2,2048]{3,2,1,0:T(2,128)(2,1)} copy(bf16[1,128,2,2048]{3,1,2,0:T(8,128)(2,1)S(1)} %get-tuple-element.8) | data formatting | bytes 2097152 | tf_op jit(solution)/shard_map/slice | solution.py:101
  48.8 1.5 %reshape_squeeze.6 = bf16[256,2048]{1,0:T(8,128)(2,1)S(1)} reshape(bf16[1,128,2,2048]{3,2,1,0:T(2,128)(2,1)} %copy.53) | data formatting | bytes 2097152 | tf_op jit(solution)/shard_map/reshape;squeeze | solution.py:101
  50.3 3.3 %copy.55 = bf16[1,128,2,2048]{3,2,1,0:T(2,128)(2,1)} copy(bf16[1,128,2,2048]{3,1,2,0:T(8,128)(2,1)} %get-tuple-element.7) | data formatting | bytes 2097152 | tf_op jit(solution)/shard_map/slice | solution.py:102
  53.6 2.2 %reshape_squeeze.7 = bf16[256,2048]{1,0:T(8,128)(2,1)} reshape(bf16[1,128,2,2048]{3,2,1,0:T(2,128)(2,1)} %copy.55) | data formatting | bytes 2097152 | tf_op jit(solution)/shard_map/reshape;squeeze | solution.py:102
  55.8 0.0 copy-start.2
  55.8 0.0 copy-start.4
  55.8 2.3 %fusion.14 = f32[256,384]{1,0:T(8,128)S(1)} fusion(bf16[256,2048]{1,0:T(8,128)(2,1)S(1)} %reshape_squeeze.6, bf16[1,2048,384]{2,1,0:T(8,128)(2,1)} %param.11), kind=kOutput, calls=%fused_computation.29 | convolution fusion | flops 402653184 | bytes 3014656 | tf_op jit(solution)/shard_map/dot_general | solution.py:53
  58.1 0.0 copy-done.2
  58.1 0.0 copy-done.4
  58.1 0.7 fusion.7
  58.9 0.0 copy-done
  58.9 0.0 copy-start.3
  58.9 0.8 multiply_convert_fusion.2
  59.7 0.6 copy-done.3
  60.3 0.7 fusion.12
  61.0 2.1 %convolution_add_fusion = f32[256,2048]{1,0:T(8,128)} fusion(f32[256,2048]{1,0:T(8,128)S(1)} %fusion.12, bf16[256,384]{1,0:T(8,128)(2,1)S(1)} %get-tuple-element.19, bf16[1,2048,384]{2,1,0:T(8,128)(2,1)S(1)} %copy-done), kind=kOutput, calls=%fused_computation.5 | convolution fusion | flops 403177472 | bytes 5963776 | tf_op jit(solution)/shard_map/dot_general | solution.py:41
  63.1 3.5 %stack_reshape.4 = f32[1,128,2,2048]{3,2,1,0:T(2,128)} reshape(f32[256,2048]{1,0:T(8,128)} %convolution_add_fusion) | data formatting | bytes 4194304 | tf_op jit(solution)/shard_map/stack;reshape | solution.py:107
  66.6 4.1 %copy.56 = f32[1,128,2,2048]{3,1,2,0:T(8,128)} copy(f32[1,128,2,2048]{3,2,1,0:T(2,128)} %stack_reshape.4) | data formatting | bytes 4194304 | tf_op jit(solution)/shard_map/stack;reshape | solution.py:107
  70.7 0.1 reshape.47
  70.8 0.0 copy-start.1
  70.8 2.3 %convolution_bitcast_fusion = f32[1,128,2,2048]{3,1,2,0:T(8,128)S(1)} fusion(bf16[1,384,2048]{2,1,0:T(8,128)(2,1)} %param.13, bf16[128,2,384]{2,1,0:T(2,128)(2,1)S(1)} %reshape.47), kind=kOutput, calls=%fused_computation.6 | convolution fusion | flops 402653184 | bytes 3866624 | tf_op jit(solution)/shard_map/dot_general | solution.py:57
  73.1 0.0 copy-done.1
  73.1 0.3 broadcast_select_fusion
  73.3 0.5 collective-permute-start.1
  73.8 3.8 %collective-permute-done.1 = f32[2,128,1,2048]{3,1,2,0:T(8,128)S(1)} collective-permute-done((f32[2,128,1,2048]{3,1,2,0:T(8,128)S(1)}, f32[2,128,1,2048]{3,1,2,0:T(8,128)S(1)}, u32[]{:S(2)}, u32[]{:S(2)}) %collective-permute-start.1) | collective-permute-done | bytes 2097184 | tf_op jit(solution)/shard_map/ppermute | solution.py:23
  77.6 0.6 add_convert_fusion
  78.2 0.1 slice_bitcast_fusion.1
  78.3 0.1 pad_maximum_fusion.4
  78.4 2.1 %copy.57 = bf16[128,2,2048]{2,1,0:T(2,128)(2,1)} copy(bf16[128,2,2048]{2,0,1:T(8,128)(2,1)S(1)} %pad_maximum_fusion.4) | data formatting | bytes 2097152 | tf_op jit(solution)/shard_map/concatenate | solution.py:10
  80.5 4.9 %all-to-all-start.1 = ((bf16[128,2,2048]{2,1,0:T(2,128)(2,1)}), bf16[128,2,2048]{2,1,0:T(2,128)(2,1)}, u32[]{:S(2)}, u32[]{:S(2)}) async-start(bf16[128,2,2048]{2,1,0:T(2,128)(2,1)} %copy.57), calls=%async_computation.1 | async-start | bytes 2097152 | tf_op jit(solution)/shard_map/all_to_all | solution.py:12
  85.4 3.0 %fusion.2 = bf16[1,384,2048]{2,1,0:T(8,128)(2,1)} fusion(bf16[256,384]{1,0:T(8,128)(2,1)S(1)} %get-tuple-element.17, bf16[256,2048]{1,0:T(8,128)(2,1)} %reshape_squeeze.7), kind=kOutput, calls=%fused_computation.9 | convolution fusion | flops 403439616 | bytes 2818048 | tf_op jit(solution)/shard_map/dot_general | solution.py:47
  88.4 1.9 %fusion = bf16[1,2048,384]{2,1,0:T(8,128)(2,1)} fusion(bf16[256,2048]{1,0:T(8,128)(2,1)S(1)} %reshape_squeeze.6, bf16[256,384]{1,0:T(8,128)(2,1)S(1)} %get-tuple-element.18), kind=kOutput, calls=%fused_computation.7 | convolution fusion | flops 403439616 | bytes 2818048 | tf_op jit(solution)/shard_map/dot_general | solution.py:47
  90.3 1.9 %fusion.1 = bf16[1,2048,384]{2,1,0:T(8,128)(2,1)} fusion(bf16[256,2048]{1,0:T(8,128)(2,1)S(1)} %reshape_squeeze.6, bf16[256,384]{1,0:T(8,128)(2,1)S(1)} %get-tuple-element.19), kind=kOutput, calls=%fused_computation.8 | convolution fusion | flops 403439616 | bytes 2818048 | tf_op jit(solution)/shard_map/dot_general | solution.py:47
  92.2 12.0 %all-to-all-done.1 = bf16[128,2,2048]{2,1,0:T(2,128)(2,1)} async-done(((bf16[128,2,2048]{2,1,0:T(2,128)(2,1)}), bf16[128,2,2048]{2,1,0:T(2,128)(2,1)}, u32[]{:S(2)}, u32[]{:S(2)}) %all-to-all-start.1) | async-done | bytes 1048608 | tf_op jit(solution)/shard_map/all_to_all | solution.py:12
  104.2 3.3 %fusion.21 = (bf16[128,1,2048]{2,1,0:T(2,128)(2,1)S(1)}, bf16[128,1,2048]{2,1,0:T(2,128)(2,1)S(1)}) fusion(bf16[128,2,2048]{2,1,0:T(2,128)(2,1)} %all-to-all-done.1), kind=kLoop, calls=%fused_computation.59 | loop fusion | bytes 2097152 | tf_op jit(solution)/shard_map/slice | solution.py:17
  107.5 1.0 convolution_convert_fusion.5
  108.5 1.2 %convolution_convert_fusion.6 = bf16[16,2048]{1,0:T(8,128)(2,1)} fusion(f32[16,128]{1,0:T(8,128)S(1)} %get-tuple-element.6, bf16[128,1,2048]{2,1,0:T(2,128)(2,1)S(1)} %get-tuple-element.12), kind=kOutput, calls=%fused_computation.15 | convolution fusion | flops 50364416 | bytes 598016 | tf_op jit(solution)/shard_map/ts,sd->td/dot_general | solution.py:124
  (1 shorter events, 0.0 us)
Async XLA Ops:
  0.6 58.2 %copy-start = (bf16[1,2048,384]{2,1,0:T(8,128)(2,1)S(1)}, bf16[1,2048,384]{2,1,0:T(8,128)(2,1)}, u32[]{:S(2)}) copy-start(bf16[1,2048,384]{2,1,0:T(8,128)(2,1)} %param.12) | copy-start | bytes 4718596
  40.3 3.9 %collective-permute-start = (bf16[2,128,1,2048]{3,1,2,0:T(8,128)(2,1)}, bf16[2,128,1,2048]{3,1,2,0:T(8,128)(2,1)}, u32[]{:S(2)}, u32[]{:S(2)}) collective-permute-start(bf16[2,128,1,2048]{3,1,2,0:T(8,128)(2,1)} %pad_maximum_fusion.3), channel_id=1, source_target_pairs={{0,1},{1,0},{2,3},{3,2},{4,5},{5,4},{6,7},{7,6},{8,9},{9,8},{10,11... | collective-permute-start | bytes 3145736 | tf_op jit(solution)/shard_map/ppermute | solution.py:23
  55.8 2.3 %copy-start.2 = (bf16[256,2048]{1,0:T(8,128)(2,1)S(1)}, bf16[256,2048]{1,0:T(8,128)(2,1)}, u32[]{:S(2)}) copy-start(bf16[256,2048]{1,0:T(8,128)(2,1)} %reshape_squeeze.7) | copy-start | bytes 3145732
  55.8 2.3 %copy-start.4 = (bf16[1,384,2048]{2,1,0:T(8,128)(2,1)S(1)}, bf16[1,384,2048]{2,1,0:T(8,128)(2,1)}, u32[]{:S(2)}) copy-start(bf16[1,384,2048]{2,1,0:T(8,128)(2,1)} %param.13) | copy-start | bytes 4718596
  58.9 1.4 %copy-start.3 = (bf16[1,2048,384]{2,1,0:T(8,128)(2,1)S(1)}, bf16[1,2048,384]{2,1,0:T(8,128)(2,1)}, u32[]{:S(2)}) copy-start(bf16[1,2048,384]{2,1,0:T(8,128)(2,1)} %param.11) | copy-start | bytes 4718596
  70.8 2.3 %copy-start.1 = (f32[1,128,2,2048]{3,1,2,0:T(8,128)S(1)}, f32[1,128,2,2048]{3,1,2,0:T(8,128)}, u32[]{:S(2)}) copy-start(f32[1,128,2,2048]{3,1,2,0:T(8,128)} %copy.56) | copy-start | bytes 6291460
  73.3 4.2 %collective-permute-start.1 = (f32[2,128,1,2048]{3,1,2,0:T(8,128)S(1)}, f32[2,128,1,2048]{3,1,2,0:T(8,128)S(1)}, u32[]{:S(2)}, u32[]{:S(2)}) collective-permute-start(f32[2,128,1,2048]{3,1,2,0:T(8,128)S(1)} %broadcast_select_fusion), channel_id=1, source_target_pairs={{0,1},{1,0},{2,3},{3,2},{4,5},{5,4},{6,7},{7,6},{8,9},{9,8},{10,11... | collective-permute-start | bytes 6291464 | tf_op jit(solution)/shard_map/ppermute | solution.py:23
  80.5 23.7 %all-to-all-start.1 = ((bf16[128,2,2048]{2,1,0:T(2,128)(2,1)}), bf16[128,2,2048]{2,1,0:T(2,128)(2,1)}, u32[]{:S(2)}, u32[]{:S(2)}) async-start(bf16[128,2,2048]{2,1,0:T(2,128)(2,1)} %copy.57), calls=%async_computation.1 | async-start | bytes 2097152 | tf_op jit(solution)/shard_map/all_to_all | solution.py:12
where the time goes:
time: 110 us
  blocking collectives  30.3 us (28%)
  local copies, waits for them, and re-layouts  27.8 us (25%)
  matrix products  20.4 us (19%)
  waiting for transfers between devices  18.4 us (17%)
  starting transfers between devices  6.67 us (6%)
  other arithmetic  5.22 us (5%)
    all_to_all x1, blocking collectives, sent_together(): lax.all_to_all(both, axis, split_axis=split_dim, concat_axis=concat_dim,...  30.3 us
    all_to_all x1, waiting for transfers between devices, sent_together(): lax.all_to_all(both, axis, split_axis=split_dim, concat_axis=concat_dim,...  12 us
    another operation x2, local copies, waits for them, and re-layouts, body(): jnp.stack((out_part.reshape(devices, capacity, feature_width), cot_part.r...  7.6 us
    dot_general x3, matrix products, contract_first(): lax.dot_general(left, right, (((0,), (0,)), ((), ())), preferred_element_...  6.74 us
    ppermute x2, waiting for transfers between devices, from_partner(): lax.ppermute(x, axis, [(i, i ^ 1 << apart) for i in range(lax.axis_size(a...  6.42 us
    all_to_all x1, starting transfers between devices, sent_together(): lax.all_to_all(both, axis, split_axis=split_dim, concat_axis=concat_dim,...  4.91 us
    slice x2, local copies, waits for them, and re-layouts, sent_together(): lax.slice_in_dim(result, at, at + a.shape[along], axis=along)  4.77 us
    dot_general x3, matrix products, contract_last(): lax.dot_general(left, right, (((1,), (1,)), ((), ())), preferred_element_...  3.54 us
  transfers between devices with their start and end apart: 3, of which 3 were waited for; matrix products, arithmetic and copies ran while one was open for 6% of the time, Pallas kernels for 0%

commit v1 on v0

v1 whole, which is shorter than its diff:
```python
import functools

import jax
import jax.numpy as jnp
from jax import lax
from jax.experimental import pallas as pl
from jax.experimental.pallas import tpu as pltpu
from jax.sharding import PartitionSpec as P


BF = jnp.bfloat16
F32 = jnp.float32
MESH = pl.DeviceIdType.MESH
GROUPS = (1, 3, 0, 2)


def dot(a, b):
    return jnp.dot(a, b, preferred_element_type=F32)


def dot_nt(a, b):
    return lax.dot_general(a, b, (((1,), (1,)), ((), ())), preferred_element_type=F32)


def dot_tn(a, b):
    return lax.dot_general(a, b, (((0,), (0,)), ((), ())), preferred_element_type=F32)


def iota(shape, dim):
    return lax.broadcasted_iota(jnp.int32, shape, dim)


def exchange(
    route_h, probs_h, tok_h, cot_h, wg_h, wu_h, wd_h,
    back, sel_t, g_gate, g_up, g_down,
    route_v, probs_v, tok_v, cot_v, wgu, wd, perm, perm_t, sel, parts, send, got,
    got_other, xt, xc, act, gu, mine, theirs, given, summed, ret,
    hsem, ss, rs, lsem, ps, pr,
):
    dp, ex = lax.axis_index("dp"), lax.axis_index("expert")
    x, y, z, c = lax.rem(dp, 4), dp // 4, ex // 2, lax.rem(ex, 2)

    def device(dx, dy, dz):
        return (
            lax.rem(y + dy + 4, 4) * 4 + lax.rem(x + dx + 4, 4),
            lax.rem(z + dz + 4, 4) * 2 + c,
        )

    def chip(dx, dy, dz):
        return (
            lax.rem(y + dy + 4, 4) * 16
            + lax.rem(x + dx + 4, 4) * 4
            + lax.rem(z + dz + 4, 4)
        )

    other = (dp, z * 2 + 1 - c)
    me = chip(0, 0, 0)

    barrier = pltpu.get_barrier_semaphore()

    def far(v):
        return lax.rem(2 + v, 4) + (v // 2) * (1 - 2 * lax.rem(v, 2))

    def greet(i, carry):
        there = device(far(lax.rem(i, 4)), far(lax.rem(i // 4, 4)), far(i // 16))
        pl.semaphore_signal(barrier, 1, device_id=there, device_id_type=MESH)
        return carry

    lax.fori_loop(0, 63, greet, 0)
    pl.semaphore_signal(barrier, 1, device_id=other, device_id_type=MESH)

    loads = [
        pltpu.make_async_copy(route_h, route_v, hsem.at[0]),
        pltpu.make_async_copy(probs_h, probs_v, hsem.at[1]),
        pltpu.make_async_copy(tok_h, tok_v, hsem.at[2]),
        pltpu.make_async_copy(cot_h, cot_v, hsem.at[3]),
        pltpu.make_async_copy(wg_h.at[0], wgu.at[:, pl.ds(0, 384)], hsem.at[4]),
        pltpu.make_async_copy(wu_h.at[0], wgu.at[:, pl.ds(384, 384)], hsem.at[5]),
        pltpu.make_async_copy(wd_h.at[0], wd, hsem.at[6]),
    ]
    for load in loads:
        load.start()

    def where_from(o):
        return (o // 2 % 16) * 16 + (o // 64) * 4 + (o // 32 % 2) * 2 + o % 2

    rows, cols = iota((256, 256), 0), iota((256, 256), 1)
    perm[...] = jnp.where(cols == where_from(rows), 1.0, 0.0).astype(BF)
    perm_t[...] = jnp.where(rows == where_from(cols), 1.0, 0.0).astype(BF)

    loads[0].wait()
    loads[1].wait()
    route, probs = route_v[...], probs_v[...]
    lane = iota((16, 128), 1)
    hits = jnp.zeros((16, 128), F32)
    weights = jnp.zeros((16, 128), F32)
    for k in range(8):
        same = route[:, k : k + 1] == lane % 64
        hits = hits + jnp.where(same, 1.0, 0.0)
        weights = weights + jnp.where(same, probs[:, k : k + 1], 0.0)
    earlier = jnp.where(iota((16, 16), 1) < iota((16, 16), 0), 1.0, 0.0).astype(BF)
    before = dot(earlier, hits.astype(BF)).astype(jnp.int32)
    slot = jnp.where(before == lane // 64, hits, 0.0)
    weights = weights * slot
    high = weights.astype(BF)
    rest = weights - high.astype(F32)
    middle = rest.astype(BF)
    low = (rest - middle.astype(F32)).astype(BF)
    spread = jnp.concatenate([slot.astype(BF), high, middle, low] * 4, axis=0)

    loads[2].wait()
    loads[3].wait()
    for q in range(4):
        quarter = slice(q * 512, (q + 1) * 512)
        parts[q * 64 : q * 64 + 16, :] = tok_v[:, quarter]
        for a in range(1, 4):
            parts[q * 64 + a * 16 : q * 64 + a * 16 + 16, :] = cot_v[:, quarter]

    for block in range(4):
        row = iota((256, 128), 0) + block * 256
        lane = iota((256, 128), 1)
        place = (row // 16 == lane % 64) & (row % 2 == lane // 64)
        picked = dot_nt(jnp.where(place, 1.0, 0.0).astype(BF), spread)
        row, col = iota((256, 256), 0), iota((256, 256), 1)
        right = (row // 4 % 4 == col // 64) & (
            (row // 2 % 2 == 1) == (col // 16 % 4 != 0)
        )
        picked = jnp.where(right, picked, 0.0)
        here = slice(block * 256, (block + 1) * 256)
        sel[here, :] = picked.astype(BF)
        send[here, :] = dot(sel[here, :], parts[...]).astype(BF)
        sel_t[:, here] = picked.T.astype(BF)

    pl.semaphore_wait(barrier, 64)

    def out_unit(group, i, sem):
        d = (i // 4, GROUPS[group], lax.rem(i, 4))
        pltpu.make_async_remote_copy(
            send.at[pl.ds(pl.multiple_of(chip(*d) * 16, 16), 16)],
            got.at[pl.ds(pl.multiple_of(group * 256 + i * 16, 16), 16)],
            ss.at[sem], rs.at[sem], device_id=device(*d), device_id_type=MESH,
        ).start()

    def back_unit(group, i, sem):
        d = (-(i // 4), -GROUPS[group], -lax.rem(i, 4))
        pltpu.make_async_remote_copy(
            ret.at[pl.ds(pl.multiple_of(group * 256 + i * 16, 16), 16)],
            back.at[pl.ds(pl.multiple_of(me * 16, 16), 16)],
            ss.at[sem], rs.at[sem], device_id=device(*d), device_id_type=MESH,
        ).start()

    def all_units(unit, chunk, sem):
        def step(j, carry):
            i = 15 - j
            unit(2 * chunk + 1, i, sem)
            if chunk == 0:
                unit(0, i, sem)
            else:

                @pl.when(i > 0)
                def _():
                    unit(2, i, sem)

            return carry

        lax.fori_loop(0, 16, step, 0)

    def landed(chunk, ref, sem):
        whole = ref.at[pl.ds(0, (32 - chunk) * 16)]
        pltpu.make_async_copy(whole, whole, sem).wait()

    all_units(out_unit, 0, 0)
    all_units(out_unit, 1, 1)
    own = pl.ds(pl.multiple_of(me * 16, 16), 16)
    own_out = pltpu.make_async_copy(send.at[own], got.at[pl.ds(512, 16)], lsem.at[0])
    own_out.start()
    own_back = pltpu.make_async_copy(ret.at[pl.ds(512, 16)], back.at[own], lsem.at[1])

    def to_other(src, dst, sem):
        return pltpu.make_async_remote_copy(
            src, dst, ps.at[sem], pr.at[sem], device_id=other, device_id_type=MESH
        )

    def unpack(src, chunk, first):
        for g in range(2):
            at = chunk * 512 + g * 256
            got_rows = dot(perm[...], src[at : at + 256, :]).astype(BF)
            to = slice(first + g * 32, first + g * 32 + 32)
            for q in range(4):
                quarter = slice(q * 512, (q + 1) * 512)
                xt[to, quarter] = got_rows[q * 64 : q * 64 + 32, :]
                xc[to, quarter] = got_rows[q * 64 + 32 : q * 64 + 64, :]

    for chunk in range(2):
        half = pl.ds(chunk * 512, 512)
        landed(chunk, got, rs.at[chunk])
        if chunk == 1:
            own_out.wait()
        share = to_other(got.at[half], got_other.at[half], chunk)
        share.start()
        unpack(got, chunk, chunk * 128)
        share.wait_recv()
        unpack(got_other, chunk, chunk * 128 + 64)
        if chunk == 0:
            for load in loads[4:]:
                load.wait()

        here = slice(chunk * 128, chunk * 128 + 128)
        gate_up = dot(xt[here, :], wgu[...])
        gate, up = gate_up[:, :384], gate_up[:, 384:]
        act_cot = dot_nt(xc[here, :], wd[...])
        sig = jax.nn.sigmoid(gate)
        act[here, :] = (gate * sig * up).astype(BF)
        gu[here, :384] = (act_cot * up * sig * (1.0 + gate * (1.0 - sig))).astype(BF)
        gu[here, 384:] = (act_cot * gate * sig).astype(BF)

        gives = []
        for q in range(4):
            quarter = slice(q * 512, (q + 1) * 512)
            cot_q = dot_nt(gu[here, :], wgu[quarter, :])
            out_q = dot(act[here, :], wd[:, quarter])
            for g in range(2):
                for a, value in enumerate((cot_q, out_q)):
                    to = q * 128 + g * 64 + a * 32
                    mine[to : to + 32, :] = value[g * 32 : g * 32 + 32, :]
                    theirs[chunk * 512 + to : chunk * 512 + to + 32, :] = value[
                        64 + g * 32 : 96 + g * 32, :
                    ].astype(BF)
            piece = pl.ds(chunk * 512 + q * 128, 128)
            give = to_other(theirs.at[piece], given.at[piece], 2 + chunk)
            give.start()
            gives.append(give)
        whole = given.at[half]
        pltpu.make_async_copy(whole, whole, pr.at[2 + chunk]).wait()

        summed[...] = (mine[...] + given[chunk * 512 : chunk * 512 + 512, :].astype(F32)).astype(BF)
        for g in range(2):
            rows_g = jnp.concatenate(
                [summed[q * 128 + g * 64 : q * 128 + g * 64 + 64, :] for q in range(4)], axis=0
            )
            at = chunk * 512 + g * 256
            ret[at : at + 256, :] = dot(perm_t[...], rows_g).astype(BF)
        all_units(back_unit, chunk, 2 + chunk)
        if chunk == 1:
            own_back.start()

    def in_grads(i, carry):
        at = pl.ds(pl.multiple_of(i * 256, 256), 256)
        both = dot_tn(xt[:, at], gu[...])
        g_gate[at, :] = both[:, :384].astype(BF)
        g_up[at, :] = both[:, 384:].astype(BF)
        return carry

    lax.fori_loop(0, 8, in_grads, 0)

    def down_grads(i, carry):
        at = pl.ds(pl.multiple_of(i * 512, 512), 512)
        g_down[:, at] = dot_tn(act[...], xc[:, at]).astype(BF)
        return carry

    lax.fori_loop(0, 4, down_grads, 0)

    for chunk in range(2):
        landed(chunk, back, rs.at[2 + chunk])
        landed(chunk, send, ss.at[chunk])
        landed(chunk, ret, ss.at[2 + chunk])
        half = pl.ds(chunk * 512, 512)
        for ref, sem in ((got, ps.at[chunk]), (theirs, ps.at[2 + chunk])):
            pltpu.make_async_copy(ref.at[half], ref.at[half], sem).wait()
    own_back.wait()


def combine(back, sel_t, g_gate, g_up, g_down, mixed, token_grad, o_gate, o_up, o_down, sems):
    stores = [
        pltpu.make_async_copy(g_gate, o_gate.at[0], sems.at[0]),
        pltpu.make_async_copy(g_up, o_up.at[0], sems.at[1]),
        pltpu.make_async_copy(g_down, o_down.at[0], sems.at[2]),
    ]
    for store in stores:
        store.start()
    both = dot(sel_t[...], back[...])
    for q in range(4):
        quarter = slice(q * 512, (q + 1) * 512)
        at = q * 64
        token_grad[:, quarter] = both[at : at + 16, :].astype(BF)
        mixed[:, quarter] = (
            both[at + 16 : at + 32, :] + both[at + 32 : at + 48, :] + both[at + 48 : at + 64, :]
        ).astype(BF)
    for store in stores:
        store.wait()


def body(tokens, route, probs, cotangent, gate_weight, up_weight, down_weight):
    any_spec = pl.BlockSpec(memory_space=pl.ANY)
    vmem_spec = pl.BlockSpec(memory_space=pltpu.VMEM)
    kept = pl.pallas_call(
        exchange,
        name="exchange",
        out_shape=[
            pltpu.VMEM((1024, 512), BF),
            pltpu.VMEM((256, 1024), BF),
            pltpu.VMEM((2048, 384), BF),
            pltpu.VMEM((2048, 384), BF),
            pltpu.VMEM((384, 2048), BF),
        ],
        in_specs=[any_spec] * 7,
        out_specs=[vmem_spec] * 5,
        scratch_shapes=[
            pltpu.VMEM((16, 8), jnp.int32),
            pltpu.VMEM((16, 8), F32),
            pltpu.VMEM((16, 2048), BF),
            pltpu.VMEM((16, 2048), BF),
            pltpu.VMEM((2048, 768), BF),
            pltpu.VMEM((384, 2048), BF),
            pltpu.VMEM((256, 256), BF),
            pltpu.VMEM((256, 256), BF),
            pltpu.VMEM((1024, 256), BF),
            pltpu.VMEM((256, 512), BF),
            pltpu.VMEM((1024, 512), BF),
            pltpu.VMEM((1024, 512), BF),
            pltpu.VMEM((1024, 512), BF),
            pltpu.VMEM((256, 2048), BF),
            pltpu.VMEM((256, 2048), BF),
            pltpu.VMEM((256, 384), BF),
            pltpu.VMEM((256, 768), BF),
            pltpu.VMEM((512, 512), F32),
            pltpu.VMEM((1024, 512), BF),
            pltpu.VMEM((1024, 512), BF),
            pltpu.VMEM((512, 512), BF),
            pltpu.VMEM((1024, 512), BF),
            pltpu.SemaphoreType.DMA((7,)),
            pltpu.SemaphoreType.DMA((4,)),
            pltpu.SemaphoreType.DMA((4,)),
            pltpu.SemaphoreType.DMA((2,)),
            pltpu.SemaphoreType.DMA((4,)),
            pltpu.SemaphoreType.DMA((4,)),
        ],
        compiler_params=pltpu.CompilerParams(
            collective_id=0, has_side_effects=True, vmem_limit_bytes=40 << 20
        ),
    )(route, probs, tokens, cotangent, gate_weight, up_weight, down_weight)
    return pl.pallas_call(
        combine,
        name="combine",
        out_shape=[
            jax.ShapeDtypeStruct(tokens.shape, BF),
            jax.ShapeDtypeStruct(tokens.shape, BF),
            jax.ShapeDtypeStruct(gate_weight.shape, BF),
            jax.ShapeDtypeStruct(up_weight.shape, BF),
            jax.ShapeDtypeStruct(down_weight.shape, BF),
        ],
        in_specs=[vmem_spec] * 5,
        out_specs=[vmem_spec] * 2 + [any_spec] * 3,
        scratch_shapes=[pltpu.SemaphoreType.DMA((3,))],
        compiler_params=pltpu.CompilerParams(vmem_limit_bytes=16 << 20),
    )(*kept)


def solution(mesh):
    rows = P(("dp", "expert"), None)
    slices = P(("dp", "expert"), None, None)
    return jax.shard_map(
        body,
        mesh=mesh,
        in_specs=(rows, rows, rows, rows, slices, slices, slices),
        out_specs=(rows, rows, slices, slices, slices),
        check_vma=False,
    )
```

time: 110 us -> 54.9 us (0.50)
  Pallas kernels: 0 us -> 45.8 us
  blocking collectives: 30.3 us -> 0 us
  matrix products: 20.4 us -> 0 us
  local copies, waits for them, and re-layouts: 27.8 us -> 7.42 us
  waiting for transfers between devices: 18.4 us -> 0 us
  starting transfers between devices: 6.67 us -> 0 us
  other arithmetic: 5.22 us -> 0 us
    pallas_call x0 -> x2, Pallas kernels: none -> 45.8 us  [the longest x1 42.8 us: body(): pl.pallas_call(exchange, name='exchange', out_shape=[pltpu.VMEM((1024, 51...]
    all_to_all x1 -> x0, blocking collectives: 30.3 us -> none  [sent_together(): lax.all_to_all(both, axis, split_axis=split_dim, concat_axis=concat_dim,...]
    dot_general x13 -> x0, matrix products: 20.4 us -> none  [the longest x3 6.74 us: contract_first(): lax.dot_general(left, right, (((0,), (0,)), ((), ())), preferred_element_...]
    all_to_all x1 -> x0, waiting for transfers between devices: 12 us -> none  [sent_together(): lax.all_to_all(both, axis, split_axis=split_dim, concat_axis=concat_dim,...]
    another operation x6 -> x0, local copies, waits for them, and re-layouts: 12 us -> none  [the longest x2 7.6 us: body(): jnp.stack((out_part.reshape(devices, capacity, feature_width), cot_part.r...]
    slice x4 -> x0, local copies, waits for them, and re-layouts: 10.1 us -> none  [the longest x2 4.77 us: sent_together(): lax.slice_in_dim(result, at, at + a.shape[along], axis=along)]
    ppermute x2 -> x0, waiting for transfers between devices: 6.42 us -> none  [from_partner(): lax.ppermute(x, axis, [(i, i ^ 1 << apart) for i in range(lax.axis_size(a...]
    unnamed x12, local copies, waits for them, and re-layouts: 2.24 us -> 7.42 us
  transfers between devices with their start and end apart: 3 -> 0, of which waited for: 3 -> 0; matrix products, arithmetic and copies ran while one was open for 6% -> 0% of each run, Pallas kernels for 0% -> 0%
where the time goes in v1:
time: 54.9 us; the launch traced here: 53.8 us
  Pallas kernels  45.8 us (83%)
  local copies, waits for them, and re-layouts  7.42 us (14%)
  between operations  0.65 us (1%)
    pallas_call x1, Pallas kernels, body(): pl.pallas_call(exchange, name='exchange', out_shape=[pltpu.VMEM((1024, 51...  42.8 us
    unnamed x12, local copies, waits for them, and re-layouts  7.42 us
    pallas_call x1, Pallas kernels, body(): pl.pallas_call(combine, name='combine', out_shape=[jax.ShapeDtypeStruct(t...  2.95 us

profile of v1, /device:TPU:1, one launch (start us, length us, event | category | flops | bytes accessed | tf_op | source)
XLA Modules:
  0.0 53.8 jit_solution(15644094704765447427)
XLA Ops:
  0.6 0.8 %copy.12.route_h = s32[16,8]{1,0:T(8,128)S(1)} copy(s32[16,8]{0,1:T(8,128)} %param.8) | data formatting | bytes 1024 | tf_op args[1]
  1.4 0.8 %copy.13.probs_h = f32[16,8]{1,0:T(8,128)S(1)} copy(f32[16,8]{0,1:T(8,128)} %param.9) | data formatting | bytes 1024 | tf_op args[2]
  2.1 0.0 copy-start
  2.1 1.4 %copy-done = bf16[1,2048,384]{2,1,0:T(8,128)(2,1)S(1)} copy-done((bf16[1,2048,384]{2,1,0:T(8,128)(2,1)S(1)}, bf16[1,2048,384]{2,1,0:T(8,128)(2,1)}, u32[]{:S(2)}) %copy-start) | copy-done | bytes 1572888
  3.6 0.0 copy-start.1
  3.6 1.4 %copy-done.1 = bf16[1,2048,384]{2,1,0:T(8,128)(2,1)S(1)} copy-done((bf16[1,2048,384]{2,1,0:T(8,128)(2,1)S(1)}, bf16[1,2048,384]{2,1,0:T(8,128)(2,1)}, u32[]{:S(2)}) %copy-start.1) | copy-done | bytes 1572888
  5.0 0.0 copy-start.2
  5.0 1.4 %copy-done.2 = bf16[1,384,2048]{2,1,0:T(8,128)(2,1)S(1)} copy-done((bf16[1,384,2048]{2,1,0:T(8,128)(2,1)S(1)}, bf16[1,384,2048]{2,1,0:T(8,128)(2,1)}, u32[]{:S(2)}) %copy-start.2) | copy-done | bytes 1572888
  6.4 0.0 copy-start.3
  6.4 0.8 %copy-done.3 = bf16[16,2048]{1,0:T(8,128)(2,1)S(1)} copy-done((bf16[16,2048]{1,0:T(8,128)(2,1)S(1)}, bf16[16,2048]{1,0:T(8,128)(2,1)}, u32[]{:S(2)}) %copy-start.3) | copy-done | bytes 65560
  7.2 0.0 copy-start.4
  7.2 0.8 %copy-done.4 = bf16[16,2048]{1,0:T(8,128)(2,1)S(1)} copy-done((bf16[16,2048]{1,0:T(8,128)(2,1)S(1)}, bf16[16,2048]{1,0:T(8,128)(2,1)}, u32[]{:S(2)}) %copy-start.4) | copy-done | bytes 65560
  8.1 42.8 %exchange.1 = (bf16[1024,512]{1,0:T(8,128)(2,1)S(1)}, bf16[256,1024]{1,0:T(8,128)(2,1)S(1)}, bf16[2048,384]{1,0:T(8,128)(2,1)S(1)}, bf16[2048,384]{1,0:T(8,128)(2,1)S(1)}, bf16[384,2048]{1,0:T(8,128)(2,1)S(1)}) custom-call(s32[16,8]{1,0:T(8,128)S(1)} %copy.12.route_h, f32[16,8]{1,0:T(8,128)S(1)} %copy.13.probs_h, bf16[16,2048]{1,0:T(8,128)(2,1)S(1)} %copy-done.3, ...), custom_call_target="tpu_custom_call" | custom-call | tf_op jit(solution)/shard_map/exchange/pallas_call | solution.py:296
  50.9 2.9 %combine.1 = (bf16[16,2048]{1,0:T(8,128)(2,1)}, bf16[16,2048]{1,0:T(8,128)(2,1)}, bf16[1,2048,384]{2,1,0:T(8,128)(2,1)}, bf16[1,2048,384]{2,1,0:T(8,128)(2,1)}, bf16[1,384,2048]{2,1,0:T(8,128)(2,1)}) custom-call(bf16[1024,512]{1,0:T(8,128)(2,1)S(1)} %get-tuple-element.10.back, bf16[256,1024]{1,0:T(8,128)(2,1)S(1)} %get-tuple-element.11.sel_t, ...), custom_call_target="tpu_custom_call" | custom-call | tf_op jit(solution)/shard_map/combine/pallas_call | solution.py:342
Async XLA Ops:
  2.1 1.4 %copy-start = (bf16[1,2048,384]{2,1,0:T(8,128)(2,1)S(1)}, bf16[1,2048,384]{2,1,0:T(8,128)(2,1)}, u32[]{:S(2)}) copy-start(bf16[1,2048,384]{2,1,0:T(8,128)(2,1)} %wg_h.1) | copy-start | bytes 4718596
  3.6 1.4 %copy-start.1 = (bf16[1,2048,384]{2,1,0:T(8,128)(2,1)S(1)}, bf16[1,2048,384]{2,1,0:T(8,128)(2,1)}, u32[]{:S(2)}) copy-start(bf16[1,2048,384]{2,1,0:T(8,128)(2,1)} %wu_h.1) | copy-start | bytes 4718596
  5.0 1.4 %copy-start.2 = (bf16[1,384,2048]{2,1,0:T(8,128)(2,1)S(1)}, bf16[1,384,2048]{2,1,0:T(8,128)(2,1)}, u32[]{:S(2)}) copy-start(bf16[1,384,2048]{2,1,0:T(8,128)(2,1)} %wd_h.1) | copy-start | bytes 4718596
  6.4 0.8 %copy-start.3 = (bf16[16,2048]{1,0:T(8,128)(2,1)S(1)}, bf16[16,2048]{1,0:T(8,128)(2,1)}, u32[]{:S(2)}) copy-start(bf16[16,2048]{1,0:T(8,128)(2,1)} %tok_h.1) | copy-start | bytes 196612
  7.2 0.8 %copy-start.4 = (bf16[16,2048]{1,0:T(8,128)(2,1)S(1)}, bf16[16,2048]{1,0:T(8,128)(2,1)}, u32[]{:S(2)}) copy-start(bf16[16,2048]{1,0:T(8,128)(2,1)} %cot_h.1) | copy-start | bytes 196612

commit v2 on v1

v2 whole, which is shorter than its diff:
```python
import functools

import jax
import jax.numpy as jnp
from jax import lax
from jax.experimental import pallas as pl
from jax.experimental.pallas import tpu as pltpu
from jax.sharding import PartitionSpec as P


BF = jnp.bfloat16
F32 = jnp.float32
MESH = pl.DeviceIdType.MESH
CHUNKS = ((0, 1), (2, 3))


def dot(a, b):
    return jnp.dot(a, b, preferred_element_type=F32)


def dot_nt(a, b):
    return lax.dot_general(a, b, (((1,), (1,)), ((), ())), preferred_element_type=F32)


def dot_tn(a, b):
    return lax.dot_general(a, b, (((0,), (0,)), ((), ())), preferred_element_type=F32)


def iota(shape, dim):
    return lax.broadcasted_iota(jnp.int32, shape, dim)


def exchange(
    route_h, probs_h, tok_h, cot_h, wg_h, wu_h, wd_h,
    back, sel_t, g_gate, g_up, g_down,
    route_v, probs_v, tok_v, cot_v, wgu, wd, wgu_t, wd_t, perm, perm_t, sel, parts, send, got,
    got_other, xt, xc, act, gu, mine, theirs, given, ret,
    hsem, ss, rs, lsem, ps, pr,
):
    dp, ex = lax.axis_index("dp"), lax.axis_index("expert")
    x, y, z, c = lax.rem(dp, 4), dp // 4, ex // 2, lax.rem(ex, 2)

    xs = [lax.rem(x + d, 4) for d in range(4)]
    ys = [lax.rem(y + d, 4) for d in range(4)]
    zs = [lax.rem(z + d, 4) for d in range(4)]
    x4s, y4s = [v * 4 for v in xs], [v * 4 for v in ys]
    z2s = [v * 2 + c for v in zs]
    x64s, y256s, z16s = [v * 64 for v in xs], [v * 256 for v in ys], [v * 16 for v in zs]

    def device(dx, dy, dz):
        return (y4s[dy % 4] + xs[dx % 4], z2s[dz % 4])

    def chip_rows(dx, dy, dz):
        row = y256s[dy % 4] + x64s[dx % 4] + z16s[dz % 4]
        return pl.ds(pl.multiple_of(row, 16), 16)

    other = (dp, z * 2 + 1 - c)
    own = chip_rows(0, 0, 0)

    barrier = pltpu.get_barrier_semaphore()

    far = sorted(
        ((dx, dy, dz) for dx in range(4) for dy in range(4) for dz in range(4)),
        key=lambda d: -sum(min(v, 4 - v) for v in d),
    )
    for d in far[:63]:
        pl.semaphore_signal(barrier, 1, device_id=device(*d), device_id_type=MESH)
    pl.semaphore_signal(barrier, 1, device_id=other, device_id_type=MESH)

    loads = [
        pltpu.make_async_copy(route_h, route_v, hsem.at[0]),
        pltpu.make_async_copy(probs_h, probs_v, hsem.at[1]),
        pltpu.make_async_copy(tok_h, tok_v, hsem.at[2]),
        pltpu.make_async_copy(cot_h, cot_v, hsem.at[3]),
        pltpu.make_async_copy(wg_h.at[0], wgu.at[:, pl.ds(0, 384)], hsem.at[4]),
        pltpu.make_async_copy(wu_h.at[0], wgu.at[:, pl.ds(384, 384)], hsem.at[5]),
        pltpu.make_async_copy(wd_h.at[0], wd, hsem.at[6]),
    ]
    for load in loads:
        load.start()

    def where_from(o):
        return (o // 2 % 16) * 16 + (o // 64) * 4 + (o // 32 % 2) * 2 + o % 2

    rows, cols = iota((256, 256), 0), iota((256, 256), 1)
    perm[...] = jnp.where(cols == where_from(rows), 1.0, 0.0).astype(BF)
    perm_t[...] = jnp.where(rows == where_from(cols), 1.0, 0.0).astype(BF)

    loads[0].wait()
    loads[1].wait()
    route, probs = route_v[...].T, probs_v[...].T
    lane = iota((16, 128), 1)
    hits = jnp.zeros((16, 128), F32)
    weights = jnp.zeros((16, 128), F32)
    for k in range(8):
        same = route[:, k : k + 1] == lane % 64
        hits = hits + jnp.where(same, 1.0, 0.0)
        weights = weights + jnp.where(same, probs[:, k : k + 1], 0.0)
    earlier = jnp.where(iota((16, 16), 1) < iota((16, 16), 0), 1.0, 0.0).astype(BF)
    before = dot(earlier, hits.astype(BF)).astype(jnp.int32)
    slot = jnp.where(before == lane // 64, hits, 0.0)
    weights = weights * slot
    high = weights.astype(BF)
    rest = weights - high.astype(F32)
    middle = rest.astype(BF)
    low = (rest - middle.astype(F32)).astype(BF)
    spread = jnp.concatenate([slot.astype(BF), high, middle, low] * 4, axis=0)

    loads[2].wait()
    loads[3].wait()
    for q in range(4):
        quarter = slice(q * 512, (q + 1) * 512)
        parts[q * 64 : q * 64 + 16, :] = tok_v[:, quarter]
        for a in range(1, 4):
            parts[q * 64 + a * 16 : q * 64 + a * 16 + 16, :] = cot_v[:, quarter]

    for block in range(4):
        row = iota((256, 128), 0) + block * 256
        lane = iota((256, 128), 1)
        place = (row // 16 == lane % 64) & (row % 2 == lane // 64)
        picked = dot_nt(jnp.where(place, 1.0, 0.0).astype(BF), spread)
        row, col = iota((256, 256), 0), iota((256, 256), 1)
        right = (row // 4 % 4 == col // 64) & (
            (row // 2 % 2 == 1) == (col // 16 % 4 != 0)
        )
        picked = jnp.where(right, picked, 0.0)
        here = slice(block * 256, (block + 1) * 256)
        sel[here, :] = picked.astype(BF)
        send[here, :] = dot(sel[here, :], parts[...]).astype(BF)
        sel_t[:, here] = picked.T.astype(BF)

    pl.semaphore_wait(barrier, 64)

    def displacement(group, i):
        dx, dz = i // 4, i % 4
        return dx, (group - dx - dz) % 4, dz

    def out_unit(group, i):
        d = displacement(group, i)
        pltpu.make_async_remote_copy(
            send.at[chip_rows(*d)],
            got.at[pl.ds(group * 256 + i * 16, 16)],
            ss.at[group], rs.at[group], device_id=device(*d), device_id_type=MESH,
        ).start()

    def back_unit(group, i):
        dx, dy, dz = displacement(group, i)
        pltpu.make_async_remote_copy(
            ret.at[pl.ds(group * 256 + i * 16, 16)],
            back.at[own],
            ss.at[4 + group], rs.at[4 + group],
            device_id=device(-dx, -dy, -dz), device_id_type=MESH,
        ).start()

    def all_units(unit, group):
        for i in reversed(range(16)):
            if group or i:
                unit(group, i)

    def landed(group, ref, sem):
        whole = ref.at[pl.ds(0, 256 if group else 240)]
        pltpu.make_async_copy(whole, whole, sem).wait()

    for group in range(4):
        all_units(out_unit, group)
    own_out = pltpu.make_async_copy(send.at[own], got.at[pl.ds(0, 16)], lsem.at[0])
    own_out.start()
    own_back = pltpu.make_async_copy(ret.at[pl.ds(0, 16)], back.at[own], lsem.at[1])

    for load in loads[4:]:
        load.wait()

    def transpose(i, carry):
        at = pl.ds(pl.multiple_of(i * 256, 256), 256)
        wgu_t[:, at] = wgu[at, :].T
        wd_t[at, :] = wd[:, at].T
        return carry

    lax.fori_loop(0, 8, transpose, 0)

    def to_other(src, dst, sem):
        return pltpu.make_async_remote_copy(
            src, dst, ps.at[sem], pr.at[sem], device_id=other, device_id_type=MESH
        )

    def unpack(src, group, first):
        at = group * 256
        got_rows = dot(perm[...], src[at : at + 256, :]).astype(BF)
        to = slice(first, first + 32)
        for q in range(4):
            quarter = slice(q * 512, (q + 1) * 512)
            xt[to, quarter] = got_rows[q * 64 : q * 64 + 32, :]
            xc[to, quarter] = got_rows[q * 64 + 32 : q * 64 + 64, :]

    def share(group):
        at = pl.ds(group * 256, 256)
        return to_other(got.at[at], got_other.at[at], group)

    def arrive(chunk):
        groups = CHUNKS[chunk]
        first = groups[0] * 64
        for group in groups:
            landed(group, got, rs.at[group])
            if group == 0:
                own_out.wait()
            share(group).start()
        for n, group in enumerate(groups):
            unpack(got, group, first + n * 32)

    def work(chunk):
        groups = CHUNKS[chunk]
        count = len(groups)
        first, half = groups[0] * 64, count * 32
        for n, group in enumerate(groups):
            share(group).wait_recv()
            unpack(got_other, group, first + half + n * 32)
        here = slice(first, first + 2 * half)
        gate_up = dot(xt[here, :], wgu[...])
        gate, up = gate_up[:, :384], gate_up[:, 384:]
        act_cot = dot(xc[here, :], wd_t[...])
        sig = jax.nn.sigmoid(gate)
        act[here, :] = (gate * sig * up).astype(BF)
        gu[here, :384] = (act_cot * up * sig * (1.0 + gate * (1.0 - sig))).astype(BF)
        gu[here, 384:] = (act_cot * gate * sig).astype(BF)
        base, size = groups[0] * 256, count * 64
        for pair in range(2):
            columns = slice(pair * 1024, (pair + 1) * 1024)
            cot_half = dot(gu[here, :], wgu_t[:, columns])
            out_half = dot(act[here, :], wd[:, columns])
            for q in (pair * 2, pair * 2 + 1):
                quarter = slice((q % 2) * 512, (q % 2) * 512 + 512)
                for n in range(count):
                    for a, value in enumerate((cot_half[:, quarter], out_half[:, quarter])):
                        to = base + q * size + n * 64 + a * 32
                        at = n * 32
                        mine[to : to + 32, :] = value[at : at + 32, :]
                        theirs[to : to + 32, :] = value[half + at : half + at + 32, :].astype(BF)
            piece = pl.ds(base + pair * 2 * size, 2 * size)
            to_other(theirs.at[piece], given.at[piece], 4 + chunk).start()

    def finish(chunk):
        groups = CHUNKS[chunk]
        count = len(groups)
        base, size = groups[0] * 256, count * 64
        whole = given.at[pl.ds(base, count * 256)]
        pltpu.make_async_copy(whole, whole, pr.at[4 + chunk]).wait()
        for n, group in enumerate(groups):
            pieces = []
            for q in range(4):
                at = base + q * size + n * 64
                pieces.append(
                    (mine[at : at + 64, :] + given[at : at + 64, :].astype(F32)).astype(BF)
                )
            back_rows = dot(perm_t[...], jnp.concatenate(pieces, axis=0)).astype(BF)
            ret[group * 256 : group * 256 + 256, :] = back_rows
        for group in groups:
            all_units(back_unit, group)
            if group == 0:
                own_back.start()

    def in_grads(i, carry):
        at = pl.ds(pl.multiple_of(i * 256, 256), 256)
        both = dot_tn(xt[:, at], gu[...])
        g_gate[at, :] = both[:, :384].astype(BF)
        g_up[at, :] = both[:, 384:].astype(BF)
        return carry

    def down_grads(i, carry):
        at = pl.ds(pl.multiple_of(i * 512, 512), 512)
        g_down[:, at] = dot_tn(act[...], xc[:, at]).astype(BF)
        return carry

    for chunk in range(len(CHUNKS)):
        arrive(chunk)
        if chunk:
            finish(chunk - 1)
        work(chunk)
    lax.fori_loop(0, 4, down_grads, 0)
    finish(len(CHUNKS) - 1)
    lax.fori_loop(0, 8, in_grads, 0)

    for group in range(4):
        landed(group, back, rs.at[4 + group])
        landed(group, send, ss.at[group])
        landed(group, ret, ss.at[4 + group])
        share(group).wait_send()
    for chunk, groups in enumerate(CHUNKS):
        whole = theirs.at[pl.ds(0, len(groups) * 256)]
        pltpu.make_async_copy(whole, whole, ps.at[4 + chunk]).wait()
    own_back.wait()


def combine(
    back, sel_t, g_gate, g_up, g_down,
    o_mixed, o_token, o_gate, o_up, o_down, mixed, token_grad, sems,
):
    stores = [
        pltpu.make_async_copy(src, dst, sems.at[n])
        for n, (src, dst) in enumerate((
            (g_gate, o_gate.at[0]), (g_up, o_up.at[0]), (g_down, o_down.at[0]),
            (mixed, o_mixed), (token_grad, o_token),
        ))
    ]
    for store in stores[:3]:
        store.start()
    both = dot(sel_t[...], back[...])
    for q in range(4):
        quarter = slice(q * 512, (q + 1) * 512)
        at = q * 64
        token_grad[:, quarter] = both[at : at + 16, :].astype(BF)
        mixed[:, quarter] = (
            both[at + 16 : at + 32, :] + both[at + 32 : at + 48, :] + both[at + 48 : at + 64, :]
        ).astype(BF)
    for store in stores[3:]:
        store.start()
    for store in stores:
        store.wait()


def body(tokens, route, probs, cotangent, gate_weight, up_weight, down_weight):
    hbm_spec = pl.BlockSpec(memory_space=pltpu.HBM)
    vmem_spec = pl.BlockSpec(memory_space=pltpu.VMEM)
    kept = pl.pallas_call(
        exchange,
        name="exchange",
        out_shape=[
            pltpu.VMEM((1024, 512), BF),
            pltpu.VMEM((256, 1024), BF),
            pltpu.VMEM((2048, 384), BF),
            pltpu.VMEM((2048, 384), BF),
            pltpu.VMEM((384, 2048), BF),
        ],
        in_specs=[hbm_spec] * 7,
        out_specs=[vmem_spec] * 5,
        scratch_shapes=[
            pltpu.VMEM((8, 16), jnp.int32),
            pltpu.VMEM((8, 16), F32),
            pltpu.VMEM((16, 2048), BF),
            pltpu.VMEM((16, 2048), BF),
            pltpu.VMEM((2048, 768), BF),
            pltpu.VMEM((384, 2048), BF),
            pltpu.VMEM((768, 2048), BF),
            pltpu.VMEM((2048, 384), BF),
            pltpu.VMEM((256, 256), BF),
            pltpu.VMEM((256, 256), BF),
            pltpu.VMEM((1024, 256), BF),
            pltpu.VMEM((256, 512), BF),
            pltpu.VMEM((1024, 512), BF),
            pltpu.VMEM((1024, 512), BF),
            pltpu.VMEM((1024, 512), BF),
            pltpu.VMEM((256, 2048), BF),
            pltpu.VMEM((256, 2048), BF),
            pltpu.VMEM((256, 384), BF),
            pltpu.VMEM((256, 768), BF),
            pltpu.VMEM((1024, 512), F32),
            pltpu.VMEM((1024, 512), BF),
            pltpu.VMEM((1024, 512), BF),
            pltpu.VMEM((1024, 512), BF),
            pltpu.SemaphoreType.DMA((7,)),
            pltpu.SemaphoreType.DMA((8,)),
            pltpu.SemaphoreType.DMA((8,)),
            pltpu.SemaphoreType.DMA((2,)),
            pltpu.SemaphoreType.DMA((8,)),
            pltpu.SemaphoreType.DMA((8,)),
        ],
        compiler_params=pltpu.CompilerParams(
            collective_id=0, has_side_effects=True, vmem_limit_bytes=60751872
        ),
    )(route.T, probs.T, tokens, cotangent, gate_weight, up_weight, down_weight)
    return pl.pallas_call(
        combine,
        name="combine",
        out_shape=[
            jax.ShapeDtypeStruct(tokens.shape, BF),
            jax.ShapeDtypeStruct(tokens.shape, BF),
            jax.ShapeDtypeStruct(gate_weight.shape, BF),
            jax.ShapeDtypeStruct(up_weight.shape, BF),
            jax.ShapeDtypeStruct(down_weight.shape, BF),
        ],
        in_specs=[vmem_spec] * 5,
        out_specs=[hbm_spec] * 5,
        scratch_shapes=[
            pltpu.VMEM(tokens.shape, BF),
            pltpu.VMEM(tokens.shape, BF),
            pltpu.SemaphoreType.DMA((5,)),
        ],
        compiler_params=pltpu.CompilerParams(vmem_limit_bytes=16 << 20),
    )(*kept)


def solution(mesh):
    rows = P(("dp", "expert"), None)
    slices = P(("dp", "expert"), None, None)
    return jax.shard_map(
        body,
        mesh=mesh,
        in_specs=(rows, rows, rows, rows, slices, slices, slices),
        out_specs=(rows, rows, slices, slices, slices),
        check_vma=False,
    )
```

time: 54.9 us -> 43.2 us (0.79); the launches traced: 53.8 us -> 43.1 us
  local copies, waits for them, and re-layouts: 7.42 us -> 0 us
  Pallas kernels: 45.8 us -> 42.5 us
    unnamed x12 -> x0, local copies, waits for them, and re-layouts: 7.42 us -> none
    pallas_call x1, Pallas kernels: 42.8 us -> 40.2 us  [body(): pl.pallas_call(exchange, name='exchange', out_shape=[pltpu.VMEM((1024, 51...]
    pallas_call x1, Pallas kernels: 2.95 us -> 2.26 us  [body(): pl.pallas_call(combine, name='combine', out_shape=[jax.ShapeDtypeStruct(t...]
where the time goes in v2:
time: 43.2 us; the launch traced here: 43.1 us
  Pallas kernels  42.5 us (98%)
  between operations  0.64 us (1%)
    pallas_call x1, Pallas kernels, body(): pl.pallas_call(exchange, name='exchange', out_shape=[pltpu.VMEM((1024, 51...  40.2 us
    pallas_call x1, Pallas kernels, body(): pl.pallas_call(combine, name='combine', out_shape=[jax.ShapeDtypeStruct(t...  2.26 us

profile of v2, /device:TPU:1, one launch (start us, length us, event | category | flops | bytes accessed | tf_op | source)
XLA Modules:
  0.0 43.1 jit_solution(2028023988821637851)
XLA Ops:
  0.6 40.2 %exchange.1 = (bf16[1024,512]{1,0:T(8,128)(2,1)S(1)}, bf16[256,1024]{1,0:T(8,128)(2,1)S(1)}, bf16[2048,384]{1,0:T(8,128)(2,1)S(1)}, bf16[2048,384]{1,0:T(8,128)(2,1)S(1)}, bf16[384,2048]{1,0:T(8,128)(2,1)S(1)}) custom-call(s32[8,16]{1,0:T(8,128)} %bitcast.2, f32[8,16]{1,0:T(8,128)} %bitcast.3, bf16[16,2048]{1,0:T(8,128)(2,1)} %tok_h.1, ...), custom_call_target="tpu_custom_call" | custom-call | tf_op jit(solution)/shard_map/exchange/pallas_call | solution.py:323
  40.9 2.3 %combine.1 = (bf16[16,2048]{1,0:T(8,128)(2,1)}, bf16[16,2048]{1,0:T(8,128)(2,1)}, bf16[1,2048,384]{2,1,0:T(8,128)(2,1)}, bf16[1,2048,384]{2,1,0:T(8,128)(2,1)}, bf16[1,384,2048]{2,1,0:T(8,128)(2,1)}) custom-call(bf16[1024,512]{1,0:T(8,128)(2,1)S(1)} %get-tuple-element.10.back, bf16[256,1024]{1,0:T(8,128)(2,1)S(1)} %get-tuple-element.11.sel_t, ...), custom_call_target="tpu_custom_call" | custom-call | tf_op jit(solution)/shard_map/combine/pallas_call | solution.py:370

commit v3 on v2

--- a/solution.py
+++ b/solution.py
@@ -11,7 +11,19 @@
 BF = jnp.bfloat16
 F32 = jnp.float32
 MESH = pl.DeviceIdType.MESH
-CHUNKS = ((0, 1), (2, 3))
+TURN = (0, 1, 2, 3)
+
+
+def hops(d):
+    return sum(min(v, 4 - v) for v in d)
+
+
+ORDER = sorted(
+    ((dx, dy, dz) for dx in range(4) for dy in range(4) for dz in range(4)),
+    key=lambda d: (TURN.index(sum(d) % 4), -hops(d), d),
+)
+HOME = ORDER.index((0, 0, 0))
+CHUNKS = ((0,), (1,), (2,), (3,))
 
 
 def dot(a, b):
@@ -59,11 +71,7 @@
 
     barrier = pltpu.get_barrier_semaphore()
 
-    far = sorted(
-        ((dx, dy, dz) for dx in range(4) for dy in range(4) for dz in range(4)),
-        key=lambda d: -sum(min(v, 4 - v) for v in d),
-    )
-    for d in far[:63]:
+    for d in sorted(ORDER, key=hops, reverse=True)[:63]:
         pl.semaphore_signal(barrier, 1, device_id=device(*d), device_id_type=MESH)
     pl.semaphore_signal(barrier, 1, device_id=other, device_id_type=MESH)
 
@@ -131,12 +139,8 @@
 
     pl.semaphore_wait(barrier, 64)
 
-    def displacement(group, i):
-        dx, dz = i // 4, i % 4
-        return dx, (group - dx - dz) % 4, dz
-
     def out_unit(group, i):
-        d = displacement(group, i)
+        d = ORDER[group * 16 + i]
         pltpu.make_async_remote_copy(
             send.at[chip_rows(*d)],
             got.at[pl.ds(group * 256 + i * 16, 16)],
@@ -144,7 +148,7 @@
         ).start()
 
     def back_unit(group, i):
-        dx, dy, dz = displacement(group, i)
+        dx, dy, dz = ORDER[group * 16 + i]
         pltpu.make_async_remote_copy(
             ret.at[pl.ds(group * 256 + i * 16, 16)],
             back.at[own],
@@ -153,19 +157,19 @@
         ).start()
 
     def all_units(unit, group):
-        for i in reversed(range(16)):
-            if group or i:
+        for i in range(16):
+            if group * 16 + i != HOME:
                 unit(group, i)
 
     def landed(group, ref, sem):
-        whole = ref.at[pl.ds(0, 256 if group else 240)]
+        whole = ref.at[pl.ds(0, 240 if group == HOME // 16 else 256)]
         pltpu.make_async_copy(whole, whole, sem).wait()
 
     for group in range(4):
         all_units(out_unit, group)
-    own_out = pltpu.make_async_copy(send.at[own], got.at[pl.ds(0, 16)], lsem.at[0])
+    own_out = pltpu.make_async_copy(send.at[own], got.at[pl.ds(HOME * 16, 16)], lsem.at[0])
     own_out.start()
-    own_back = pltpu.make_async_copy(ret.at[pl.ds(0, 16)], back.at[own], lsem.at[1])
+    own_back = pltpu.make_async_copy(ret.at[pl.ds(HOME * 16, 16)], back.at[own], lsem.at[1])
 
     for load in loads[4:]:
         load.wait()
@@ -198,16 +202,18 @@
 
     def arrive(chunk):
         groups = CHUNKS[chunk]
-        first = groups[0] * 64
         for group in groups:
             landed(group, got, rs.at[group])
-            if group == 0:
+            if group == HOME // 16:
                 own_out.wait()
             share(group).start()
+
+    def open_own(chunk):
+        groups = CHUNKS[chunk]
         for n, group in enumerate(groups):
-            unpack(got, group, first + n * 32)
-
-    def work(chunk):
+            unpack(got, group, groups[0] * 64 + n * 32)
+
+    def first_half(chunk):
         groups = CHUNKS[chunk]
         count = len(groups)
         first, half = groups[0] * 64, count * 32
@@ -222,6 +228,12 @@
         act[here, :] = (gate * sig * up).astype(BF)
         gu[here, :384] = (act_cot * up * sig * (1.0 + gate * (1.0 - sig))).astype(BF)
         gu[here, 384:] = (act_cot * gate * sig).astype(BF)
+
+    def second_half(chunk):
+        groups = CHUNKS[chunk]
+        count = len(groups)
+        first, half = groups[0] * 64, count * 32
+        here = slice(first, first + 2 * half)
         base, size = groups[0] * 256, count * 64
         for pair in range(2):
             columns = slice(pair * 1024, (pair + 1) * 1024)
@@ -255,7 +267,7 @@
             ret[group * 256 : group * 256 + 256, :] = back_rows
         for group in groups:
             all_units(back_unit, group)
-            if group == 0:
+            if group == HOME // 16:
                 own_back.start()
 
     def in_grads(i, carry):
@@ -270,11 +282,17 @@
         g_down[:, at] = dot_tn(act[...], xc[:, at]).astype(BF)
         return carry
 
+    arrive(0)
+    open_own(0)
     for chunk in range(len(CHUNKS)):
-        arrive(chunk)
+        first_half(chunk)
         if chunk:
             finish(chunk - 1)
-        work(chunk)
+        if chunk + 1 < len(CHUNKS):
+            arrive(chunk + 1)
+        second_half(chunk)
+        if chunk + 1 < len(CHUNKS):
+            open_own(chunk + 1)
     lax.fori_loop(0, 4, down_grads, 0)
     finish(len(CHUNKS) - 1)
     lax.fori_loop(0, 8, in_grads, 0)

time: 43.2 us -> 41.7 us (0.965)
  Pallas kernels: 42.5 us -> 40.9 us
    pallas_call x1, Pallas kernels: 40.2 us -> 38.7 us  [body(): pl.pallas_call(exchange, name='exchange', out_shape=[pltpu.VMEM((1024, 51...]
where the time goes in v3:
time: 41.7 us; the launch traced here: 41.6 us
  Pallas kernels  40.9 us (98%)
  between operations  0.64 us (2%)
    pallas_call x1, Pallas kernels, body(): pl.pallas_call(exchange, name='exchange', out_shape=[pltpu.VMEM((1024, 51...  38.7 us
    pallas_call x1, Pallas kernels, body(): pl.pallas_call(combine, name='combine', out_shape=[jax.ShapeDtypeStruct(t...  2.26 us

profile of v3, /device:TPU:1, one launch (start us, length us, event | category | flops | bytes accessed | tf_op | source)
XLA Modules:
  0.0 41.6 jit_solution(12893415131047630615)
XLA Ops:
  0.6 38.7 %exchange.1 = (bf16[1024,512]{1,0:T(8,128)(2,1)S(1)}, bf16[256,1024]{1,0:T(8,128)(2,1)S(1)}, bf16[2048,384]{1,0:T(8,128)(2,1)S(1)}, bf16[2048,384]{1,0:T(8,128)(2,1)S(1)}, bf16[384,2048]{1,0:T(8,128)(2,1)S(1)}) custom-call(s32[8,16]{1,0:T(8,128)} %bitcast.2, f32[8,16]{1,0:T(8,128)} %bitcast.3, bf16[16,2048]{1,0:T(8,128)(2,1)} %tok_h.1, ...), custom_call_target="tpu_custom_call" | custom-call | tf_op jit(solution)/shard_map/exchange/pallas_call | solution.py:341
  39.3 2.3 %combine.1 = (bf16[16,2048]{1,0:T(8,128)(2,1)}, bf16[16,2048]{1,0:T(8,128)(2,1)}, bf16[1,2048,384]{2,1,0:T(8,128)(2,1)}, bf16[1,2048,384]{2,1,0:T(8,128)(2,1)}, bf16[1,384,2048]{2,1,0:T(8,128)(2,1)}) custom-call(bf16[1024,512]{1,0:T(8,128)(2,1)S(1)} %get-tuple-element.10.back, bf16[256,1024]{1,0:T(8,128)(2,1)S(1)} %get-tuple-element.11.sel_t, ...), custom_call_target="tpu_custom_call" | custom-call | tf_op jit(solution)/shard_map/combine/pallas_call | solution.py:388

commit v4 on v3

--- a/solution.py
+++ b/solution.py
@@ -11,7 +11,7 @@
 BF = jnp.bfloat16
 F32 = jnp.float32
 MESH = pl.DeviceIdType.MESH
-TURN = (0, 1, 2, 3)
+TURN = (2, 1, 3, 0)
 
 
 def hops(d):

time: 41.7 us -> 41.6 us (level)
  no operation moved by 1% of the time
where the time goes in v4:
time: 41.6 us; the launch traced here: 41.5 us
  Pallas kernels  40.9 us (98%)
  between operations  0.64 us (2%)
    pallas_call x1, Pallas kernels, body(): pl.pallas_call(exchange, name='exchange', out_shape=[pltpu.VMEM((1024, 51...  38.6 us
    pallas_call x1, Pallas kernels, body(): pl.pallas_call(combine, name='combine', out_shape=[jax.ShapeDtypeStruct(t...  2.26 us

profile of v4, /device:TPU:1, one launch (start us, length us, event | category | flops | bytes accessed | tf_op | source)
XLA Modules:
  0.0 41.5 jit_solution(16316261269242639721)
XLA Ops:
  0.6 38.6 %exchange.1 = (bf16[1024,512]{1,0:T(8,128)(2,1)S(1)}, bf16[256,1024]{1,0:T(8,128)(2,1)S(1)}, bf16[2048,384]{1,0:T(8,128)(2,1)S(1)}, bf16[2048,384]{1,0:T(8,128)(2,1)S(1)}, bf16[384,2048]{1,0:T(8,128)(2,1)S(1)}) custom-call(s32[8,16]{1,0:T(8,128)} %bitcast.2, f32[8,16]{1,0:T(8,128)} %bitcast.3, bf16[16,2048]{1,0:T(8,128)(2,1)} %tok_h.1, ...), custom_call_target="tpu_custom_call" | custom-call | tf_op jit(solution)/shard_map/exchange/pallas_call | solution.py:341
  39.3 2.3 %combine.1 = (bf16[16,2048]{1,0:T(8,128)(2,1)}, bf16[16,2048]{1,0:T(8,128)(2,1)}, bf16[1,2048,384]{2,1,0:T(8,128)(2,1)}, bf16[1,2048,384]{2,1,0:T(8,128)(2,1)}, bf16[1,384,2048]{2,1,0:T(8,128)(2,1)}) custom-call(bf16[1024,512]{1,0:T(8,128)(2,1)S(1)} %get-tuple-element.10.back, bf16[256,1024]{1,0:T(8,128)(2,1)S(1)} %get-tuple-element.11.sel_t, ...), custom_call_target="tpu_custom_call" | custom-call | tf_op jit(solution)/shard_map/combine/pallas_call | solution.py:388
